TPU v7x, 128 devices: a whole 4x4x4 slice. The times are simulated.
128 devices in a mesh: layer: 4 (over x), row: 16 (over z, y), col: 2 (over core).
Axes of the slice: x: 4, y: 4, z: 4, core: 2. Of those that a mesh axis runs over, the one named last changes fastest.
Arguments:
- density: bfloat16 [8192, 8192], P('row', 'col'), may hold values from -0.5 to 1.5
- pattern: int32 [64, 64], P('row', 'col'), may hold values from 0 to 1, as said below
- holder: int32 [4096, 1], P(('layer', 'row', 'col')), may hold values from 0 to 31; in each aligned block of 32 rows (0 to 31, 32 to 63, ...) at most 2 rows name the same one
- slot_index: int32 [4096], P(('layer', 'row', 'col')), may hold values from 0 to 31
- atom_index: int32 [4096], P(('layer', 'row', 'col')), may hold values from 0 to 7
- derivative: bfloat16 [4096, 3, 128, 128], P(('layer', 'row', 'col')), may hold values from -1.1953125 to 1.1953125
Outputs:
- forces: float32 [3, 1024], P(None, ('layer', 'row', 'col'))
Inputs may be any that keep to these rules, and one draw needn't show every extreme that they name: `pattern`: the blocks held by one (row, col) grid position form a tile of 4 x 32; in some tile every block is 1. Among the derivative blocks of one device no holder is named more than 2 times, a bound that some block reaches; every holder is named on some device.
All inputs are finite; a program needn't handle non-finite values.
Results may differ from a plain program's by a relative error of at most 0.015.
Values may be sent and summed in bfloat16 or wider, within the bound.
A program may use at most 128 MiB of HBM per device.

v0:
```python
import jax
import jax.numpy as jnp
from jax import lax
from jax.sharding import PartitionSpec as P

BS = 128
ATOM_DEV = 8


def in_order(parts, dim):
    parts = jnp.moveaxis(parts, 0, dim)
    shape = parts.shape
    return parts.reshape(*shape[:dim], shape[dim] * shape[dim + 1], *shape[dim + 2 :])


def copy_for_each(value, axis):
    length = lax.axis_size(axis)
    return lax.all_to_all(
        jnp.broadcast_to(value[None], (length, *value.shape)), axis, 0, 0, tiled=True
    )


def gathered_copies(value, axis, dim):
    return in_order(copy_for_each(value, axis), dim)


def block_filter(matrix, kept_blocks):
    count_rows, count_cols = kept_blocks.shape
    blocked = matrix.reshape(count_rows, BS, count_cols, BS)
    return jnp.where(kept_blocks[:, None, :, None], blocked, jnp.zeros_like(blocked)).reshape(
        matrix.shape
    )


def column_subset(matrix, layer_count, layer_id):
    reshaped = matrix.reshape(matrix.shape[0], -1, layer_count, BS)
    picked = lax.dynamic_index_in_dim(reshaped, layer_id, 2, keepdims=False)
    return picked.reshape(matrix.shape[0], -1)


def row_subset(matrix, layer_count, layer_id):
    reshaped = matrix.reshape(-1, layer_count, BS, matrix.shape[1])
    picked = lax.dynamic_index_in_dim(reshaped, layer_id, 1, keepdims=False)
    return picked.reshape(-1, matrix.shape[1])


def multiply(left_matrix, right_matrix, layer_count, layer_id):
    left_part = column_subset(left_matrix, layer_count, layer_id)
    right_part = row_subset(right_matrix, layer_count, layer_id)
    row_strip = lax.all_gather(right_part, "row", axis=0, tiled=True)
    return jnp.dot(
        gathered_copies(left_part, "col", 1), row_strip, preferred_element_type=jnp.float32
    )


def shards(density, pattern, holder, slot_index, atom_index, derivative):
    layer_count = lax.axis_size("layer")
    layer_id = lax.axis_index("layer")
    grid_row = lax.axis_index("row")
    grid_col = lax.axis_index("col")
    row_blocks, col_blocks = pattern.shape
    global_rows = grid_row * row_blocks + jnp.arange(row_blocks, dtype=jnp.int32)
    global_cols = grid_col * col_blocks + jnp.arange(col_blocks, dtype=jnp.int32)
    kept_blocks = (pattern == 1) | (global_rows[:, None] == global_cols[None, :])
    filtered = block_filter(density, kept_blocks)
    partial_square = multiply(filtered, filtered, layer_count, layer_id)
    share_blocks = row_blocks // layer_count
    square_share = lax.psum_scatter(
        partial_square, "layer", scatter_dimension=0, tiled=True
    ).astype(jnp.bfloat16)
    square = lax.all_gather(square_share, "layer", axis=0, tiled=True)
    partial_cube = multiply(square, filtered, layer_count, layer_id)
    cube_share = lax.psum_scatter(partial_cube, "layer", scatter_dimension=0, tiled=True)
    kept_share = lax.dynamic_slice_in_dim(kept_blocks, layer_id * share_blocks, share_blocks, 0)
    purified = block_filter(
        3.0 * square_share.astype(jnp.float32) - 2.0 * cube_share, kept_share
    ).astype(jnp.bfloat16)
    held_blocks = (
        purified.reshape(share_blocks, BS, col_blocks, BS)
        .transpose(0, 2, 1, 3)
        .reshape(share_blocks * col_blocks, BS, BS)
    )
    holders_total = lax.axis_size("row") * lax.axis_size("col")
    entry_count = slot_index.shape[0]
    capacity = max(2, 2 * entry_count // holders_total)
    targets = holder[:, 0]
    target_hot = (targets[:, None] == jnp.arange(holders_total, dtype=jnp.int32)[None, :]).astype(
        jnp.int32
    )
    rank_values = jnp.sum(target_hot * (jnp.cumsum(target_hot, axis=0) - 1), axis=1)
    positions = targets * capacity + rank_values
    position_hot = (
        positions[None, :] == jnp.arange(holders_total * capacity, dtype=jnp.int32)[:, None]
    )
    requests = jnp.sum(jnp.where(position_hot, slot_index[None, :], 0), axis=1).reshape(
        holders_total, capacity
    )
    fetched = jnp.take(
        held_blocks,
        lax.all_to_all(requests, ("row", "col"), split_axis=0, concat_axis=0, tiled=True),
        axis=0,
    )
    returned = lax.all_to_all(fetched, ("row", "col"), split_axis=0, concat_axis=0, tiled=True)
    arrived = jnp.take(returned.reshape(holders_total * capacity, BS, BS), positions, axis=0)
    contrib = jnp.einsum("eij,exij->xe", arrived, derivative, preferred_element_type=jnp.float32)
    atom_hot = (atom_index[:, None] == jnp.arange(ATOM_DEV, dtype=jnp.int32)[None, :]).astype(
        jnp.float32
    )
    return -2.0 * jnp.dot(contrib, atom_hot, precision=lax.Precision.HIGHEST)


def solution(mesh):
    return jax.shard_map(
        shards,
        mesh=mesh,
        in_specs=(
            P("row", "col"),
            P("row", "col"),
            P(("layer", "row", "col"), None),
            P(("layer", "row", "col")),
            P(("layer", "row", "col")),
            P(("layer", "row", "col"), None, None, None),
        ),
        out_specs=P(None, ("layer", "row", "col")),
        check_vma=False,
    )
```

profile of v0, /device:TPU:0, one launch (start us, length us, event | category | flops | bytes accessed | tf_op | source)
XLA Modules:
  0.0 459.0 jit_solution(10009303842181600829)
XLA Ops:
  7.6 2.3 dynamic-slice_select_fusion
  10.1 6.5 %copy.40 = bf16[512,4096]{0,1:T(8,128)(2,1)} copy(bf16[512,4096]{1,0:T(8,128)(2,1)} %param.6) | data formatting | bytes 8388608 | tf_op args[0]
  18.2 6.4 %all_to_all.30 = bf16[2,512,1024]{1,2,0:T(8,128)(2,1)} all-to-all(bf16[2,512,1024]{1,2,0:T(8,128)(2,1)S(1)} %broadcast_in_dim.109), channel_id=1, replica_groups=mesh['layer'=4,'row'=16,'col'=2] {'col'}, dimensions={0} | all-to-all | bytes 4194304 | tf_op jit(solution)/shard_map/all_to_all | solution.py:18
  24.6 99.4 %all-gather.6.cloned.1.call-done = bf16[1,1,2048,4096]{3,2,1,0:T(8,128)(2,1)} async-done(((bf16[1,1,128,4096]{3,2,1,0:T(8,128)(2,1)}), bf16[1,1,2048,4096]{3,2,1,0:T(8,128)(2,1)}) %all-gather.6.cloned.1.call-update) | async-done | bytes 16777232 | tf_op jit(solution)/shard_map/all_gather | solution.py:50
  124.0 15.1 %fusion.2 = f32[512,4096]{1,0:T(8,128)} fusion(bf16[512,2048]{0,1:T(8,128)(2,1)} %bitcast.69, bf16[1,1,2048,4096]{3,2,1,0:T(8,128)(2,1)} %all-gather.6.cloned.1.call-done), kind=kOutput, calls=%fused_computation.4 | convolution fusion | flops 8589934592 | bytes 27262976 | tf_op jit(solution)/shard_map/dot_general | solution.py:51
  139.2 80.1 %reduce-scatter.3.cloned.1.call-done = f32[128,4096]{1,0:T(8,128)} async-done(((f32[512,4096]{1,0:T(8,128)}), f32[128,4096]{1,0:T(8,128)}) %reduce-scatter.3.cloned.1.call-update) | async-done | bytes 2097168 | tf_op jit(solution)/shard_map/reduce_scatter | solution.py:68
  219.4 2.7 convert_element_type.14
  222.1 48.1 %all-gather.4.cloned.1.call-done = bf16[512,4096]{1,0:T(8,128)(2,1)} async-done(((bf16[128,4096]{1,0:T(8,128)(2,1)}), bf16[512,4096]{1,0:T(8,128)(2,1)}) %all-gather.4.cloned.1.call-update) | async-done | bytes 4194320 | tf_op jit(solution)/shard_map/all_gather | solution.py:71
  270.2 7.8 %reshape.121 = bf16[512,8,4,128]{3,2,1,0:T(4,128)(2,1)} reshape(bf16[512,4096]{1,0:T(8,128)(2,1)} %all-gather.4.cloned.1.call-done) | data formatting | bytes 8388608 | tf_op jit(solution)/shard_map/reshape | solution.py:36
  278.0 5.7 %constant_dynamic-slice_fusion = bf16[512,8,1,128]{3,2,1,0:T(2,128)(2,1)} fusion(bf16[512,8,4,128]{3,2,1,0:T(4,128)(2,1)} %reshape.121, s32[]{:T(128)S(6)} %select_n.68), kind=kLoop, calls=%fused_computation.36 | loop fusion | bytes 2097156 | tf_op jit(solution)/shard_map/jit(dynamic_index_in_dim)/dynamic_slice | solution.py:37
  283.7 5.8 %copy.48 = bf16[512,8,1,128]{0,3,1,2:T(8,128)(2,1)} copy(bf16[512,8,1,128]{3,2,1,0:T(2,128)(2,1)} %constant_dynamic-slice_fusion) | data formatting | bytes 2097152
  290.9 5.4 %all_to_all.31 = bf16[2,512,1024]{1,2,0:T(8,128)(2,1)S(1)} all-to-all(bf16[2,512,1024]{1,2,0:T(8,128)(2,1)S(1)} %broadcast_in_dim.115), channel_id=1, replica_groups=mesh['layer'=4,'row'=16,'col'=2] {'col'}, dimensions={0} | all-to-all | bytes 4194304 | tf_op jit(solution)/shard_map/all_to_all | solution.py:18
  296.3 14.5 %fusion = f32[512,4096]{1,0:T(8,128)} fusion(bf16[512,2048]{0,1:T(8,128)(2,1)S(1)} %bitcast.70, bf16[1,1,2048,4096]{3,2,1,0:T(8,128)(2,1)} %all-gather.6.cloned.1.call-done), kind=kOutput, calls=%fused_computation.2 | convolution fusion | flops 8589934592 | bytes 27262976 | tf_op jit(solution)/shard_map/dot_general | solution.py:51
  312.6 7.3 %all-to-all-start = ((s32[32,1,2]{2,1,0:T(1,128)}), s32[32,1,2]{2,1,0:T(1,128)S(1)}, u32[]{:S(2)}, u32[]{:S(2)}) async-start(s32[32,1,2]{2,1,0:T(1,128)} %bitcast.3), calls=%async_computation | async-start | bytes 32768 | tf_op jit(solution)/shard_map/all_to_all | solution.py:100
  320.0 7.3 %all-to-all-done = s32[32,1,2]{2,1,0:T(1,128)S(1)} async-done(((s32[32,1,2]{2,1,0:T(1,128)}), s32[32,1,2]{2,1,0:T(1,128)S(1)}, u32[]{:S(2)}, u32[]{:S(2)}) %all-to-all-start) | async-done | bytes 288 | tf_op jit(solution)/shard_map/all_to_all | solution.py:100
  327.6 64.2 %reduce-scatter.5.cloned.1.call-done = f32[128,4096]{1,0:T(8,128)} async-done(((f32[512,4096]{1,0:T(8,128)}), f32[128,4096]{1,0:T(8,128)}) %reduce-scatter.5.cloned.1.call-update) | async-done | bytes 2097168 | tf_op jit(solution)/shard_map/reduce_scatter | solution.py:73
  391.9 2.6 fusion.7
  394.7 1.4 copy.57
  396.2 3.4 gather_fusion
  399.6 3.2 broadcast_select_fusion
  402.7 7.4 %all-to-all-start.3 = ((bf16[32,2,128,128]{3,2,1,0:T(8,128)(2,1)}), bf16[32,2,128,128]{3,2,1,0:T(8,128)(2,1)}, u32[]{:S(2)}, u32[]{:S(2)}) async-start(bf16[32,2,128,128]{3,2,1,0:T(8,128)(2,1)} %broadcast_select_fusion), calls=%async_computation.5 | async-start | bytes 4194304 | tf_op jit(solution)/shard_map/all_to_all | solution.py:103
  410.1 29.9 %all-to-all-done.3 = bf16[32,2,128,128]{3,2,1,0:T(8,128)(2,1)} async-done(((bf16[32,2,128,128]{3,2,1,0:T(8,128)(2,1)}), bf16[32,2,128,128]{3,2,1,0:T(8,128)(2,1)}, u32[]{:S(2)}, u32[]{:S(2)}) %all-to-all-start.3) | async-done | bytes 2097184 | tf_op jit(solution)/shard_map/all_to_all | solution.py:103
  440.1 3.3 gather_fusion.1
  444.8 6.9 %fusion.4 = f32[32,1,3,1]{2,1,3,0:T(1,128)S(1)} fusion(bf16[32,3,128,128]{3,2,1,0:T(8,128)(2,1)S(1)} %copy-done, bf16[32,128,128,1]{2,1,0,3:T(8,128)(2,1)S(1)} %select_bitcast_fusion), kind=kOutput, calls=%fused_computation.6 | convolution fusion | flops 3145728 | bytes 4194688 | tf_op jit(solution)/shard_map/eij,exij->xe/dot_general | solution.py:105
  (49 shorter events, 9.0 us)
Async XLA Ops:
  6.5 438.2 %copy-start = (bf16[32,3,128,128]{3,2,1,0:T(8,128)(2,1)S(1)}, bf16[32,3,128,128]{3,2,1,0:T(8,128)(2,1)}, u32[]{:S(2)}) copy-start(bf16[32,3,128,128]{3,2,1,0:T(8,128)(2,1)} %param.11) | copy-start | bytes 9437188
  6.5 117.5 %all-gather.6.cloned.1.call-start = ((), (), s32[]{:S(2)}) async-start(), calls=%async_computation.9 | async-start | bytes 17825792 | tf_op jit(solution)/shard_map/all_gather | solution.py:50
  9.9 209.4 %reduce-scatter.3.cloned.1.call-start = ((), (), s32[]{:S(2)}) async-start(), calls=%async_computation.6 | async-start | bytes 10485760 | tf_op jit(solution)/shard_map/reduce_scatter | solution.py:68
  139.2 131.0 %all-gather.4.cloned.1.call-start = ((), (), s32[]{:S(2)}) async-start(), calls=%async_computation.7 | async-start | bytes 5242880 | tf_op jit(solution)/shard_map/all_gather | solution.py:71
  222.1 169.8 %reduce-scatter.5.cloned.1.call-start = ((), (), s32[]{:S(2)}) async-start(), calls=%async_computation.8 | async-start | bytes 10485760 | tf_op jit(solution)/shard_map/reduce_scatter | solution.py:73
  310.8 0.7 copy-start.1
  310.8 1.0 copy-start.2
  312.6 14.6 %all-to-all-start = ((s32[32,1,2]{2,1,0:T(1,128)}), s32[32,1,2]{2,1,0:T(1,128)S(1)}, u32[]{:S(2)}, u32[]{:S(2)}) async-start(s32[32,1,2]{2,1,0:T(1,128)} %bitcast.3), calls=%async_computation | async-start | bytes 32768 | tf_op jit(solution)/shard_map/all_to_all | solution.py:100
  402.7 37.4 %all-to-all-start.3 = ((bf16[32,2,128,128]{3,2,1,0:T(8,128)(2,1)}), bf16[32,2,128,128]{3,2,1,0:T(8,128)(2,1)}, u32[]{:S(2)}, u32[]{:S(2)}) async-start(bf16[32,2,128,128]{3,2,1,0:T(8,128)(2,1)} %broadcast_select_fusion), calls=%async_computation.5 | async-start | bytes 4194304 | tf_op jit(solution)/shard_map/all_to_all | solution.py:103
  444.7 6.9 %copy-start.3 = (s32[32]{0:T(128)S(1)}, s32[32]{0:T(128)}, u32[]{:S(2)}) copy-start(s32[32]{0:T(128)} %param.10) | copy-start | bytes 388
Sparse Core Ops, SparseCore 0:
  10.0 113.9 all-gather.5
  139.3 80.0 reduce-scatter.2
  222.2 47.9 all-gather.3
  311.0 80.8 reduce-scatter.4
where the time goes:
time: 460 us; the launch traced here: 459 us
  waiting for transfers between devices  329 us (72%)
  local copies, waits for them, and re-layouts  37.8 us (8%)
  matrix products  37.4 us (8%)
  starting transfers between devices  14.8 us (3%)
  other arithmetic  14.8 us (3%)
  between operations  13.3 us (3%)
  blocking collectives  11.8 us (3%)
    all_gather x1, waiting for transfers between devices, multiply(): row_strip = lax.all_gather(right_part, 'row', axis=0, tiled=True)  99.4 us
    reduce_scatter x1, waiting for transfers between devices, shards(): lax.psum_scatter(partial_square, 'layer', scatter_dimension=0, tiled=True)  80.1 us
    reduce_scatter x1, waiting for transfers between devices, shards(): lax.psum_scatter(partial_cube, 'layer', scatter_dimension=0, tiled=True)  64.2 us
    all_gather x1, waiting for transfers between devices, shards(): square = lax.all_gather(square_share, 'layer', axis=0, tiled=True)  48.1 us
    all_to_all x1, waiting for transfers between devices, shards(): lax.all_to_all(fetched, ('row', 'col'), split_axis=0, concat_axis=0, tile...  29.9 us
    dot_general x2, matrix products, multiply(): jnp.dot(gathered_copies(left_part, 'col', 1), row_strip, preferred_elemen...  29.7 us
    unnamed x13, local copies, waits for them, and re-layouts  13.3 us
    all_to_all x2, blocking collectives, copy_for_each(): lax.all_to_all(jnp.broadcast_to(value[None], (length, *value.shape)), axi...  11.8 us
  transfers between devices with their start and end apart: 6, of which 6 were waited for; matrix products, arithmetic and copies ran while one was open for 2% of the time, Pallas kernels for 0%

commit v1 on v0

--- a/solution.py
+++ b/solution.py
@@ -47,7 +47,21 @@
 def multiply(left_matrix, right_matrix, layer_count, layer_id):
     left_part = column_subset(left_matrix, layer_count, layer_id)
     right_part = row_subset(right_matrix, layer_count, layer_id)
-    row_strip = lax.all_gather(right_part, "row", axis=0, tiled=True)
+    ways, here, step = (lax.axis_size("row"), lax.axis_index("row"), right_part.shape[0])
+    shape_2 = [n * ways if d == 0 else n for d, n in enumerate(right_part.shape)]
+    full = lax.dynamic_update_slice_in_dim(
+        jnp.zeros(shape_2, right_part.dtype), right_part, here * step, axis=0
+    )
+    going_up = going_down = right_part
+    for far in range(1, ways // 2 + 1):
+        going_up = lax.ppermute(going_up, "row", [(d, (d + 1) % ways) for d in range(ways)])
+        full = lax.dynamic_update_slice_in_dim(full, going_up, (here - far) % ways * step, axis=0)
+        if 2 * far < ways:
+            going_down = lax.ppermute(going_down, "row", [(d, (d - 1) % ways) for d in range(ways)])
+            full = lax.dynamic_update_slice_in_dim(
+                full, going_down, (here + far) % ways * step, axis=0
+            )
+    row_strip = full
     return jnp.dot(
         gathered_copies(left_part, "col", 1), row_strip, preferred_element_type=jnp.float32
     )

time: 460 us -> 560 us (1.22)
  starting transfers between devices: 14.8 us -> 60.3 us
  local copies, waits for them, and re-layouts: 37.8 us -> 70 us
  waiting for transfers between devices: 329 us -> 357 us
  blocking collectives: 11.8 us -> 5.42 us
    ppermute x0 -> x15, waiting for transfers between devices: none -> 130 us  [the longest x8 79.3 us: multiply(): lax.ppermute(going_up, 'row', [(d, (d + 1) % ways) for d in range(ways)])]
    all_gather x1 -> x0, waiting for transfers between devices: 99.4 us -> none  [multiply(): row_strip = lax.all_gather(right_part, 'row', axis=0, tiled=True)]
    ppermute x0 -> x15, starting transfers between devices: none -> 40.4 us  [the longest x7 38.8 us: multiply(): lax.ppermute(going_down, 'row', [(d, (d - 1) % ways) for d in range(ways)])]
    dynamic_update_slice x0 -> x15, local copies, waits for them, and re-layouts: none -> 24.7 us  [the longest x8 13.6 us: multiply(): lax.dynamic_update_slice_in_dim(full, going_up, (here - far) % ways * ste...]
    all_to_all x2 -> x1, blocking collectives: 11.8 us -> 5.42 us  [copy_for_each(): lax.all_to_all(jnp.broadcast_to(value[None], (length, *value.shape)), axi...]
    another operation x0 -> x1, local copies, waits for them, and re-layouts: none -> 5.97 us
    unnamed x13 -> x17, local copies, waits for them, and re-layouts: 13.3 us -> 13.7 us
  transfers between devices with their start and end apart: 6 -> 21, of which waited for: 6 -> 17; matrix products, arithmetic and copies ran while one was open for 2% -> 6% of each run, Pallas kernels for 0% -> 0%
where the time goes in v1:
time: 560 us; the launch traced here: 559 us
  waiting for transfers between devices  357 us (64%)
  local copies, waits for them, and re-layouts  70 us (12%)
  starting transfers between devices  60.3 us (11%)
  matrix products  37.4 us (7%)
  other arithmetic  14.9 us (3%)
  between operations  13.6 us (2%)
    ppermute x8, waiting for transfers between devices, multiply(): lax.ppermute(going_up, 'row', [(d, (d + 1) % ways) for d in range(ways)])  79.3 us
    reduce_scatter x1, waiting for transfers between devices, shards(): lax.psum_scatter(partial_square, 'layer', scatter_dimension=0, tiled=True)  76.8 us
    reduce_scatter x1, waiting for transfers between devices, shards(): lax.psum_scatter(partial_cube, 'layer', scatter_dimension=0, tiled=True)  64.6 us
    ppermute x7, waiting for transfers between devices, multiply(): lax.ppermute(going_down, 'row', [(d, (d - 1) % ways) for d in range(ways)])  51.1 us
    all_gather x1, waiting for transfers between devices, shards(): square = lax.all_gather(square_share, 'layer', axis=0, tiled=True)  48.1 us
    ppermute x7, starting transfers between devices, multiply(): lax.ppermute(going_down, 'row', [(d, (d - 1) % ways) for d in range(ways)])  38.8 us
    all_to_all x1, waiting for transfers between devices, shards(): lax.all_to_all(fetched, ('row', 'col'), split_axis=0, concat_axis=0, tile...  29.9 us
    dot_general x2, matrix products, multiply(): jnp.dot(gathered_copies(left_part, 'col', 1), row_strip, preferred_elemen...  29.7 us
  transfers between devices with their start and end apart: 21, of which 17 were waited for; matrix products, arithmetic and copies ran while one was open for 6% of the time, Pallas kernels for 0%

profile of v1, /device:TPU:0, one launch (start us, length us, event | category | flops | bytes accessed | tf_op | source)
XLA Modules:
  0.0 558.6 jit_solution(14970949051798907830)
XLA Ops:
  7.6 6.0 %broadcast.104 = bf16[2048,4096]{1,0:T(8,128)(2,1)} broadcast(bf16[]{:T(256)} %constant.189.clone.1), dimensions={} | broadcast | bytes 16777218 | tf_op jit(solution)/shard_map/broadcast.3
  22.5 23.2 %collective-permute-done = bf16[128,4096]{1,0:T(8,128)(2,1)S(1)} collective-permute-done((bf16[128,4096]{1,0:T(8,128)(2,1)S(1)}, bf16[128,4096]{1,0:T(8,128)(2,1)S(1)}, u32[]{:S(2)}, u32[]{:S(2)}) %collective-permute-start) | collective-permute-done | bytes 1048608 | tf_op jit(solution)/shard_map/ppermute | solution.py:57
  52.0 21.4 %collective-permute-done.2 = bf16[128,4096]{1,0:T(8,128)(2,1)} collective-permute-done((bf16[128,4096]{1,0:T(8,128)(2,1)S(1)}, bf16[128,4096]{1,0:T(8,128)(2,1)}, u32[]{:S(2)}, u32[]{:S(2)}) %collective-permute-start.2) | collective-permute-done | bytes 1048608 | tf_op jit(solution)/shard_map/ppermute | solution.py:57
  73.6 5.9 %collective-permute-start.5 = (bf16[128,4096]{1,0:T(8,128)(2,1)}, bf16[128,4096]{1,0:T(8,128)(2,1)}, u32[]{:S(2)}, u32[]{:S(2)}) collective-permute-start(bf16[128,4096]{1,0:T(8,128)(2,1)} %collective-permute-done.3), channel_id=1, source_target_pairs={{0,30},{2,0},{4,2},{6,4},{8,6},{10,8},{12,10},{14,12},{16,14},{18,... | collective-permute-start | bytes 3145736 | tf_op jit(solution)/shard_map/ppermute | solution.py:60
  79.6 6.5 %copy.40 = bf16[512,4096]{0,1:T(8,128)(2,1)} copy(bf16[512,4096]{1,0:T(8,128)(2,1)} %param.6) | data formatting | bytes 8388608 | tf_op args[0]
  86.3 14.2 %collective-permute-done.4 = bf16[128,4096]{1,0:T(8,128)(2,1)} collective-permute-done((bf16[128,4096]{1,0:T(8,128)(2,1)}, bf16[128,4096]{1,0:T(8,128)(2,1)}, u32[]{:S(2)}, u32[]{:S(2)}) %collective-permute-start.4) | collective-permute-done | bytes 1048608 | tf_op jit(solution)/shard_map/ppermute | solution.py:57
  118.4 8.3 %collective-permute-done.6 = bf16[128,4096]{1,0:T(8,128)(2,1)} collective-permute-done((bf16[128,4096]{1,0:T(8,128)(2,1)}, bf16[128,4096]{1,0:T(8,128)(2,1)}, u32[]{:S(2)}, u32[]{:S(2)}) %collective-permute-start.6) | collective-permute-done | bytes 1048608 | tf_op jit(solution)/shard_map/ppermute | solution.py:57
  131.3 7.9 %collective-permute-done.7 = bf16[128,4096]{1,0:T(8,128)(2,1)S(1)} collective-permute-done((bf16[128,4096]{1,0:T(8,128)(2,1)}, bf16[128,4096]{1,0:T(8,128)(2,1)S(1)}, u32[]{:S(2)}, u32[]{:S(2)}) %collective-permute-start.7) | collective-permute-done | bytes 1048608 | tf_op jit(solution)/shard_map/ppermute | solution.py:60
  156.4 10.4 %collective-permute-done.9 = bf16[128,4096]{1,0:T(8,128)(2,1)S(1)} collective-permute-done((bf16[128,4096]{1,0:T(8,128)(2,1)S(1)}, bf16[128,4096]{1,0:T(8,128)(2,1)S(1)}, u32[]{:S(2)}, u32[]{:S(2)}) %collective-permute-start.9) | collective-permute-done | bytes 1048608 | tf_op jit(solution)/shard_map/ppermute | solution.py:60
  166.8 5.8 %collective-permute-start.11 = (bf16[128,4096]{1,0:T(8,128)(2,1)S(1)}, bf16[128,4096]{1,0:T(8,128)(2,1)S(1)}, u32[]{:S(2)}, u32[]{:S(2)}) collective-permute-start(bf16[128,4096]{1,0:T(8,128)(2,1)S(1)} %collective-permute-done.9), channel_id=1, source_target_pairs={{0,30},{2,0},{4,2},{6,4},{8,6},{10,8},{12,10},{14,12},{16,14},{18,... | collective-permute-start | bytes 3145736 | tf_op jit(solution)/shard_map/ppermute | solution.py:60
  177.9 15.7 %collective-permute-done.11 = bf16[128,4096]{1,0:T(8,128)(2,1)S(1)} collective-permute-done((bf16[128,4096]{1,0:T(8,128)(2,1)S(1)}, bf16[128,4096]{1,0:T(8,128)(2,1)S(1)}, u32[]{:S(2)}, u32[]{:S(2)}) %collective-permute-start.11) | collective-permute-done | bytes 1048608 | tf_op jit(solution)/shard_map/ppermute | solution.py:60
  202.5 16.9 %collective-permute-done.13 = bf16[128,4096]{1,0:T(8,128)(2,1)S(1)} collective-permute-done((bf16[128,4096]{1,0:T(8,128)(2,1)S(1)}, bf16[128,4096]{1,0:T(8,128)(2,1)S(1)}, u32[]{:S(2)}, u32[]{:S(2)}) %collective-permute-start.13) | collective-permute-done | bytes 1048608 | tf_op jit(solution)/shard_map/ppermute | solution.py:60
  227.1 15.1 %fusion.9 = f32[512,4096]{1,0:T(8,128)} fusion(bf16[512,2048]{0,1:T(8,128)(2,1)} %bitcast.10, bf16[2048,4096]{1,0:T(8,128)(2,1)} %constant_dynamic-update-slice_fusion), kind=kOutput, calls=%fused_computation.57 | convolution fusion | flops 8589934592 | bytes 27262976 | tf_op jit(solution)/shard_map/dot_general | solution.py:65
  242.4 76.8 %reduce-scatter.3.cloned.1.call-done = f32[128,4096]{1,0:T(8,128)} async-done(((f32[512,4096]{1,0:T(8,128)}), f32[128,4096]{1,0:T(8,128)}) %reduce-scatter.3.cloned.1.call-update) | async-done | bytes 2097168 | tf_op jit(solution)/shard_map/reduce_scatter | solution.py:82
  322.0 48.1 %all-gather.2.cloned.1.call-done = bf16[512,4096]{1,0:T(8,128)(2,1)} async-done(((bf16[128,4096]{1,0:T(8,128)(2,1)}), bf16[512,4096]{1,0:T(8,128)(2,1)}) %all-gather.2.cloned.1.call-update) | async-done | bytes 4194320 | tf_op jit(solution)/shard_map/all_gather | solution.py:85
  370.1 7.7 %reshape.121 = bf16[512,8,4,128]{3,2,1,0:T(4,128)(2,1)} reshape(bf16[512,4096]{1,0:T(8,128)(2,1)} %all-gather.2.cloned.1.call-done) | data formatting | bytes 8388608 | tf_op jit(solution)/shard_map/reshape | solution.py:36
  383.4 5.8 %copy.48 = bf16[512,8,1,128]{0,3,1,2:T(8,128)(2,1)} copy(bf16[512,8,1,128]{3,2,1,0:T(2,128)(2,1)} %constant_dynamic-slice_fusion) | data formatting | bytes 2097152
  396.1 14.6 %fusion.10 = f32[512,4096]{1,0:T(8,128)} fusion(bf16[512,2048]{0,1:T(8,128)(2,1)S(1)} %bitcast.69, bf16[2048,4096]{1,0:T(8,128)(2,1)} %constant_dynamic-update-slice_fusion), kind=kOutput, calls=%fused_computation.58 | convolution fusion | flops 8589934592 | bytes 27262976 | tf_op jit(solution)/shard_map/dot_general | solution.py:65
  411.8 7.5 %all-to-all-start = ((s32[32,1,2]{2,1,0:T(1,128)}), s32[32,1,2]{2,1,0:T(1,128)S(1)}, u32[]{:S(2)}, u32[]{:S(2)}) async-start(s32[32,1,2]{2,1,0:T(1,128)} %bitcast.3), calls=%async_computation | async-start | bytes 32768 | tf_op jit(solution)/shard_map/all_to_all | solution.py:114
  419.4 7.3 %all-to-all-done = s32[32,1,2]{2,1,0:T(1,128)S(1)} async-done(((s32[32,1,2]{2,1,0:T(1,128)}), s32[32,1,2]{2,1,0:T(1,128)S(1)}, u32[]{:S(2)}, u32[]{:S(2)}) %all-to-all-start) | async-done | bytes 288 | tf_op jit(solution)/shard_map/all_to_all | solution.py:114
  427.0 64.6 %reduce-scatter.5.cloned.1.call-done = f32[128,4096]{1,0:T(8,128)} async-done(((f32[512,4096]{1,0:T(8,128)}), f32[128,4096]{1,0:T(8,128)}) %reduce-scatter.5.cloned.1.call-update) | async-done | bytes 2097168 | tf_op jit(solution)/shard_map/reduce_scatter | solution.py:87
  502.4 7.4 %all-to-all-start.3 = ((bf16[32,2,128,128]{3,2,1,0:T(8,128)(2,1)}), bf16[32,2,128,128]{3,2,1,0:T(8,128)(2,1)}, u32[]{:S(2)}, u32[]{:S(2)}) async-start(bf16[32,2,128,128]{3,2,1,0:T(8,128)(2,1)} %broadcast_select_fusion), calls=%async_computation.5 | async-start | bytes 4194304 | tf_op jit(solution)/shard_map/all_to_all | solution.py:117
  509.8 29.9 %all-to-all-done.3 = bf16[32,2,128,128]{3,2,1,0:T(8,128)(2,1)} async-done(((bf16[32,2,128,128]{3,2,1,0:T(8,128)(2,1)}), bf16[32,2,128,128]{3,2,1,0:T(8,128)(2,1)}, u32[]{:S(2)}, u32[]{:S(2)}) %all-to-all-start.3) | async-done | bytes 2097184 | tf_op jit(solution)/shard_map/all_to_all | solution.py:117
  544.4 6.9 %fusion = f32[32,1,3,1]{2,1,3,0:T(1,128)S(1)} fusion(bf16[32,3,128,128]{3,2,1,0:T(8,128)(2,1)S(1)} %copy-done, bf16[32,128,128,1]{2,1,0,3:T(8,128)(2,1)S(1)} %select_bitcast_fusion), kind=kOutput, calls=%fused_computation.2 | convolution fusion | flops 3145728 | bytes 4194688 | tf_op jit(solution)/shard_map/eij,exij->xe/dot_general | solution.py:119
  (97 shorter events, 111.1 us)
Async XLA Ops:
  6.5 537.9 %copy-start = (bf16[32,3,128,128]{3,2,1,0:T(8,128)(2,1)S(1)}, bf16[32,3,128,128]{3,2,1,0:T(8,128)(2,1)}, u32[]{:S(2)}) copy-start(bf16[32,3,128,128]{3,2,1,0:T(8,128)(2,1)} %param.11) | copy-start | bytes 9437188
  16.0 29.7 %collective-permute-start = (bf16[128,4096]{1,0:T(8,128)(2,1)S(1)}, bf16[128,4096]{1,0:T(8,128)(2,1)S(1)}, u32[]{:S(2)}, u32[]{:S(2)}) collective-permute-start(bf16[128,4096]{1,0:T(8,128)(2,1)S(1)} %get-tuple-element.8), channel_id=1, source_target_pairs={{0,2},{2,4},{4,6},{6,8},{8,10},{10,12},{12,14},{14,16},{16,18},{18... | collective-permute-start | bytes 3145736 | tf_op jit(solution)/shard_map/ppermute | solution.py:57
  17.6 28.1 %collective-permute-start.1 = (bf16[128,4096]{1,0:T(8,128)(2,1)S(1)}, bf16[128,4096]{1,0:T(8,128)(2,1)S(1)}, u32[]{:S(2)}, u32[]{:S(2)}) collective-permute-start(bf16[128,4096]{1,0:T(8,128)(2,1)S(1)} %get-tuple-element.8), channel_id=1, source_target_pairs={{0,30},{2,0},{4,2},{6,4},{8,6},{10,8},{12,10},{14,12},{16,14},{18,... | collective-permute-start | bytes 3145736 | tf_op jit(solution)/shard_map/ppermute | solution.py:60
  45.7 27.9 %copy-start.2 = (bf16[128,4096]{1,0:T(8,128)(2,1)}, bf16[128,4096]{1,0:T(8,128)(2,1)S(1)}, u32[]{:S(2)}) copy-start(bf16[128,4096]{1,0:T(8,128)(2,1)S(1)} %collective-permute-done) | copy-start | bytes 3145732
  45.7 27.8 %collective-permute-start.2 = (bf16[128,4096]{1,0:T(8,128)(2,1)S(1)}, bf16[128,4096]{1,0:T(8,128)(2,1)}, u32[]{:S(2)}, u32[]{:S(2)}) collective-permute-start(bf16[128,4096]{1,0:T(8,128)(2,1)S(1)} %collective-permute-done), channel_id=1, source_target_pairs={{0,2},{2,4},{4,6},{6,8},{8,10},{10,12},{12,14},{14,16},{16,18},{18... | collective-permute-start | bytes 3145736 | tf_op jit(solution)/shard_map/ppermute | solution.py:57
  46.7 26.9 %collective-permute-start.3 = (bf16[128,4096]{1,0:T(8,128)(2,1)S(1)}, bf16[128,4096]{1,0:T(8,128)(2,1)}, u32[]{:S(2)}, u32[]{:S(2)}) collective-permute-start(bf16[128,4096]{1,0:T(8,128)(2,1)S(1)} %collective-permute-done.1), channel_id=1, source_target_pairs={{0,30},{2,0},{4,2},{6,4},{8,6},{10,8},{12,10},{14,12},{16,14},{18,... | collective-permute-start | bytes 3145736 | tf_op jit(solution)/shard_map/ppermute | solution.py:60
  73.4 27.1 %collective-permute-start.4 = (bf16[128,4096]{1,0:T(8,128)(2,1)}, bf16[128,4096]{1,0:T(8,128)(2,1)}, u32[]{:S(2)}, u32[]{:S(2)}) collective-permute-start(bf16[128,4096]{1,0:T(8,128)(2,1)} %collective-permute-done.2), channel_id=1, source_target_pairs={{0,2},{2,4},{4,6},{6,8},{8,10},{10,12},{12,14},{14,16},{16,18},{18... | collective-permute-start | bytes 3145736 | tf_op jit(solution)/shard_map/ppermute | solution.py:57
  73.6 37.1 %collective-permute-start.5 = (bf16[128,4096]{1,0:T(8,128)(2,1)}, bf16[128,4096]{1,0:T(8,128)(2,1)}, u32[]{:S(2)}, u32[]{:S(2)}) collective-permute-start(bf16[128,4096]{1,0:T(8,128)(2,1)} %collective-permute-done.3), channel_id=1, source_target_pairs={{0,30},{2,0},{4,2},{6,4},{8,6},{10,8},{12,10},{14,12},{16,14},{18,... | collective-permute-start | bytes 3145736 | tf_op jit(solution)/shard_map/ppermute | solution.py:60
  100.5 26.1 %collective-permute-start.6 = (bf16[128,4096]{1,0:T(8,128)(2,1)}, bf16[128,4096]{1,0:T(8,128)(2,1)}, u32[]{:S(2)}, u32[]{:S(2)}) collective-permute-start(bf16[128,4096]{1,0:T(8,128)(2,1)} %collective-permute-done.4), channel_id=1, source_target_pairs={{0,2},{2,4},{4,6},{6,8},{8,10},{10,12},{12,14},{14,16},{16,18},{18... | collective-permute-start | bytes 3145736 | tf_op jit(solution)/shard_map/ppermute | solution.py:57
  103.3 123.9 %all-to-all-start.1 = ((bf16[2,512,1024]{1,2,0:T(8,128)(2,1)}), bf16[2,512,1024]{1,2,0:T(8,128)(2,1)}, u32[]{:S(2)}, u32[]{:S(2)}) async-start(bf16[2,512,1024]{1,2,0:T(8,128)(2,1)} %broadcast_in_dim.109), calls=%async_computation.1 | async-start | bytes 4194304 | tf_op jit(solution)/shard_map/all_to_all | solution.py:18
  108.1 211.1 %reduce-scatter.3.cloned.1.call-start = ((), (), s32[]{:S(2)}) async-start(), calls=%async_computation.6 | async-start | bytes 10485760 | tf_op jit(solution)/shard_map/reduce_scatter | solution.py:82
  110.7 28.4 %collective-permute-start.7 = (bf16[128,4096]{1,0:T(8,128)(2,1)}, bf16[128,4096]{1,0:T(8,128)(2,1)S(1)}, u32[]{:S(2)}, u32[]{:S(2)}) collective-permute-start(bf16[128,4096]{1,0:T(8,128)(2,1)} %collective-permute-done.5), channel_id=1, source_target_pairs={{0,30},{2,0},{4,2},{6,4},{8,6},{10,8},{12,10},{14,12},{16,14},{18,... | collective-permute-start | bytes 3145736 | tf_op jit(solution)/shard_map/ppermute | solution.py:60
  126.6 25.1 %collective-permute-start.8 = (bf16[128,4096]{1,0:T(8,128)(2,1)}, bf16[128,4096]{1,0:T(8,128)(2,1)S(1)}, u32[]{:S(2)}, u32[]{:S(2)}) collective-permute-start(bf16[128,4096]{1,0:T(8,128)(2,1)} %collective-permute-done.6), channel_id=1, source_target_pairs={{0,2},{2,4},{4,6},{6,8},{8,10},{10,12},{12,14},{14,16},{16,18},{18... | collective-permute-start | bytes 3145736 | tf_op jit(solution)/shard_map/ppermute | solution.py:57
  139.2 27.6 %collective-permute-start.9 = (bf16[128,4096]{1,0:T(8,128)(2,1)S(1)}, bf16[128,4096]{1,0:T(8,128)(2,1)S(1)}, u32[]{:S(2)}, u32[]{:S(2)}) collective-permute-start(bf16[128,4096]{1,0:T(8,128)(2,1)S(1)} %collective-permute-done.7), channel_id=1, source_target_pairs={{0,30},{2,0},{4,2},{6,4},{8,6},{10,8},{12,10},{14,12},{16,14},{18,... | collective-permute-start | bytes 3145736 | tf_op jit(solution)/shard_map/ppermute | solution.py:60
  151.8 24.0 %collective-permute-start.10 = (bf16[128,4096]{1,0:T(8,128)(2,1)S(1)}, bf16[128,4096]{1,0:T(8,128)(2,1)S(1)}, u32[]{:S(2)}, u32[]{:S(2)}) collective-permute-start(bf16[128,4096]{1,0:T(8,128)(2,1)S(1)} %collective-permute-done.8), channel_id=1, source_target_pairs={{0,2},{2,4},{4,6},{6,8},{8,10},{10,12},{12,14},{14,16},{16,18},{18... | collective-permute-start | bytes 3145736 | tf_op jit(solution)/shard_map/ppermute | solution.py:57
  166.8 26.8 %collective-permute-start.11 = (bf16[128,4096]{1,0:T(8,128)(2,1)S(1)}, bf16[128,4096]{1,0:T(8,128)(2,1)S(1)}, u32[]{:S(2)}, u32[]{:S(2)}) collective-permute-start(bf16[128,4096]{1,0:T(8,128)(2,1)S(1)} %collective-permute-done.9), channel_id=1, source_target_pairs={{0,30},{2,0},{4,2},{6,4},{8,6},{10,8},{12,10},{14,12},{16,14},{18,... | collective-permute-start | bytes 3145736 | tf_op jit(solution)/shard_map/ppermute | solution.py:60
  175.7 24.7 %collective-permute-start.12 = (bf16[128,4096]{1,0:T(8,128)(2,1)S(1)}, bf16[128,4096]{1,0:T(8,128)(2,1)S(1)}, u32[]{:S(2)}, u32[]{:S(2)}) collective-permute-start(bf16[128,4096]{1,0:T(8,128)(2,1)S(1)} %collective-permute-done.10), channel_id=1, source_target_pairs={{0,2},{2,4},{4,6},{6,8},{8,10},{10,12},{12,14},{14,16},{16,18},{18... | collective-permute-start | bytes 3145736 | tf_op jit(solution)/shard_map/ppermute | solution.py:57
  193.6 25.9 %collective-permute-start.13 = (bf16[128,4096]{1,0:T(8,128)(2,1)S(1)}, bf16[128,4096]{1,0:T(8,128)(2,1)S(1)}, u32[]{:S(2)}, u32[]{:S(2)}) collective-permute-start(bf16[128,4096]{1,0:T(8,128)(2,1)S(1)} %collective-permute-done.11), channel_id=1, source_target_pairs={{0,30},{2,0},{4,2},{6,4},{8,6},{10,8},{12,10},{14,12},{16,14},{18,... | collective-permute-start | bytes 3145736 | tf_op jit(solution)/shard_map/ppermute | solution.py:60
  200.4 25.6 %collective-permute-start.14 = (bf16[128,4096]{1,0:T(8,128)(2,1)S(1)}, bf16[128,4096]{1,0:T(8,128)(2,1)S(1)}, u32[]{:S(2)}, u32[]{:S(2)}) collective-permute-start(bf16[128,4096]{1,0:T(8,128)(2,1)S(1)} %collective-permute-done.12), channel_id=1, source_target_pairs={{0,2},{2,4},{4,6},{6,8},{8,10},{10,12},{12,14},{14,16},{16,18},{18... | collective-permute-start | bytes 3145736 | tf_op jit(solution)/shard_map/ppermute | solution.py:57
  242.3 127.7 %all-gather.2.cloned.1.call-start = ((), (), s32[]{:S(2)}) async-start(), calls=%async_computation.7 | async-start | bytes 5242880 | tf_op jit(solution)/shard_map/all_gather | solution.py:85
  321.9 169.7 %reduce-scatter.5.cloned.1.call-start = ((), (), s32[]{:S(2)}) async-start(), calls=%async_computation.8 | async-start | bytes 10485760 | tf_op jit(solution)/shard_map/reduce_scatter | solution.py:87
  396.1 14.9 %copy-start.4 = (s32[32]{0:T(128)S(1)}, s32[32]{0:T(128)}, u32[]{:S(2)}) copy-start(s32[32]{0:T(128)} %param.9) | copy-start | bytes 388
  411.8 14.8 %all-to-all-start = ((s32[32,1,2]{2,1,0:T(1,128)}), s32[32,1,2]{2,1,0:T(1,128)S(1)}, u32[]{:S(2)}, u32[]{:S(2)}) async-start(s32[32,1,2]{2,1,0:T(1,128)} %bitcast.3), calls=%async_computation | async-start | bytes 32768 | tf_op jit(solution)/shard_map/all_to_all | solution.py:114
  502.4 37.4 %all-to-all-start.3 = ((bf16[32,2,128,128]{3,2,1,0:T(8,128)(2,1)}), bf16[32,2,128,128]{3,2,1,0:T(8,128)(2,1)}, u32[]{:S(2)}, u32[]{:S(2)}) async-start(bf16[32,2,128,128]{3,2,1,0:T(8,128)(2,1)} %broadcast_select_fusion), calls=%async_computation.5 | async-start | bytes 4194304 | tf_op jit(solution)/shard_map/all_to_all | solution.py:117
  (3 other events, 22.5 us)
Sparse Core Ops, SparseCore 0:
  242.4 76.7 reduce-scatter.2
  322.0 47.9 all-gather.1
  410.8 80.8 reduce-scatter.4
